TPU v7x, 512 devices: a whole 4x8x8 slice. The times are simulated.
512 devices in a mesh: blk: 64 (over z, y_lo, core), head: 8 (over x, y_hi).
Axes of the slice: x: 4, y: 8 (y_hi: 2, y_lo: 4; y = y_hi * 4 + y_lo), z: 8, core: 2. Of those that a mesh axis runs over, the one named last changes fastest.
Arguments:
- queries: bfloat16 [4096, 3584], P('blk', 'head'), may hold values from -64 to 64
- new_keys: bfloat16 [4096, 3584], P('blk', 'head'), may hold values from -6 to 6
- new_values: bfloat16 [4096, 3584], P('blk', 'head'), may hold values from -6 to 6
- key_cache: bfloat16 [512, 128, 3584], P('blk', None, 'head'), may hold values from -6 to 6
- value_cache: bfloat16 [512, 128, 3584], P('blk', None, 'head'), may hold values from -6 to 6
- out_weight: bfloat16 [3584, 3584], P('head'), may hold values from -0.09375 to 0.09375
- cache_len: int32 [4], replicated, may hold values from 1 to 16384, as said below
- page_table: int32 [512], replicated, may hold values from 0 to 511, each once
- block_perm: int32 [64], replicated, may hold values from 0 to 63, each once
Outputs:
- projected: bfloat16 [4096, 3584], P('blk', 'head')
Inputs may be any that keep to these rules, and one draw needn't show every extreme that they name: `cache_len`: some request has exactly 16384 cached tokens. `page_table`: each global page appears once. `block_perm`: each query block appears once.
All inputs are finite; a program needn't handle non-finite values.
Results may differ from a plain program's by a relative error of at most 0.015.
Values may be sent and summed in bfloat16 or wider, within the bound.
No kernel may reach another device: no remote copies, remote signals or barrier semaphores. Data moves between devices by JAX's collectives and lax.ppermute only.
A program may use at most 128 MiB of HBM per device.

v0:
```python
import math

import jax
import jax.numpy as jnp
from jax import lax
from jax.sharding import PartitionSpec as P

HD = 224
PAGE = 128
P_DEV = 8
NEW = 1024
TOK_DEV = 64
MAXP = 128


def block_partial(query_rows, key_rows, value_rows, visible):
    head_count = query_rows.shape[1] // HD
    query_heads = query_rows.reshape(query_rows.shape[0], head_count, HD)
    key_heads = key_rows.reshape(key_rows.shape[0], head_count, HD)
    value_heads = value_rows.reshape(value_rows.shape[0], head_count, HD)
    scores = jnp.einsum(
        "qhd,khd->hqk", query_heads, key_heads, preferred_element_type=jnp.float32
    ) * (1.0 / math.sqrt(HD))
    scores = jnp.where(visible[None], scores, -1e30)
    row_top = jnp.max(scores, axis=2)
    weights = jnp.where(visible[None], jnp.exp(scores - row_top[:, :, None]), 0.0).astype(
        jnp.bfloat16
    )
    row_sum = jnp.sum(weights.astype(jnp.float32), axis=2)
    numerators = jnp.einsum(
        "hqk,khd->qhd", weights, value_heads, preferred_element_type=jnp.float32
    )
    return (row_top.T, row_sum.T, numerators)


def absorb(carry_state, request, partial_value):
    numer_all, top_all, sum_all = carry_state
    part_top, part_sum, part_numer = partial_value
    old_top = lax.dynamic_index_in_dim(top_all, request, 0, keepdims=False)
    old_sum = lax.dynamic_index_in_dim(sum_all, request, 0, keepdims=False)
    old_numer = lax.dynamic_index_in_dim(numer_all, request, 0, keepdims=False)
    new_top = jnp.maximum(old_top, part_top)
    old_factor = jnp.exp(old_top - new_top)
    part_factor = jnp.exp(part_top - new_top)
    merged_sum = old_factor * old_sum + part_factor * part_sum
    merged_numer = old_numer * old_factor[:, :, None] + part_numer * part_factor[:, :, None]
    return (
        lax.dynamic_update_index_in_dim(numer_all, merged_numer, request, 0),
        lax.dynamic_update_index_in_dim(top_all, new_top, request, 0),
        lax.dynamic_update_index_in_dim(sum_all, merged_sum, request, 0),
    )


def shards(
    queries,
    new_keys,
    new_values,
    key_cache,
    value_cache,
    out_weight,
    cache_len,
    page_table,
    block_perm,
):
    row_width = queries.shape[1]
    head_count = row_width // HD
    blk_count = lax.axis_size("blk")
    my_index = lax.axis_index("blk")
    req_count = cache_len.shape[0]
    blocks_per_req = NEW // TOK_DEV
    gathered = lax.all_gather(queries, "blk", axis=0, tiled=True)
    block_ids = jnp.arange(blk_count, dtype=jnp.int32)
    inverse = jnp.zeros((blk_count,), jnp.int32).at[block_perm].set(block_ids)
    query_all = gathered.reshape(blk_count, TOK_DEV, row_width)[inverse].reshape(
        req_count, NEW, row_width
    )
    global_ids = my_index * P_DEV + jnp.arange(P_DEV, dtype=jnp.int32)
    table_ids = jnp.arange(page_table.shape[0], dtype=jnp.int32)
    match_rows = page_table[None, :] == global_ids[:, None]
    logical = jnp.sum(jnp.where(match_rows, table_ids[None, :], 0), axis=1)
    page_req = logical // MAXP
    page_pos = logical % MAXP
    page_fill = jnp.clip(cache_len[page_req] - page_pos * PAGE, 0, PAGE)
    slot_ids = jnp.arange(PAGE, dtype=jnp.int32)
    start_state = (
        jnp.zeros((req_count, NEW, head_count, HD), jnp.float32),
        jnp.full((req_count, NEW, head_count), -1e30, jnp.float32),
        jnp.zeros((req_count, NEW, head_count), jnp.float32),
    )

    def page_work(slot_index, carry_state):
        request = page_req[slot_index]
        query_rows = lax.dynamic_index_in_dim(query_all, request, 0, keepdims=False)
        key_rows = lax.dynamic_index_in_dim(key_cache, slot_index, 0, keepdims=False)
        value_rows = lax.dynamic_index_in_dim(value_cache, slot_index, 0, keepdims=False)
        visible = jnp.broadcast_to((slot_ids < page_fill[slot_index])[None, :], (NEW, PAGE))
        return absorb(
            carry_state, request, block_partial(query_rows, key_rows, value_rows, visible)
        )

    def page_step(slot_index, carry_state):
        return page_work(slot_index, carry_state)

    carry_state = lax.fori_loop(0, P_DEV, page_step, start_state)
    my_block = block_perm[my_index]
    my_request = my_block // blocks_per_req
    my_offset = my_block % blocks_per_req * TOK_DEV
    new_pos = jnp.arange(NEW, dtype=jnp.int32)[:, None]
    key_pos = my_offset + jnp.arange(TOK_DEV, dtype=jnp.int32)[None, :]
    own_rows = lax.dynamic_index_in_dim(query_all, my_request, 0, keepdims=False)
    carry_state = absorb(
        carry_state, my_request, block_partial(own_rows, new_keys, new_values, new_pos >= key_pos)
    )
    numer_all, top_all, sum_all = carry_state
    send_numer = numer_all.reshape(blk_count, TOK_DEV, row_width)[block_perm]
    send_top = top_all.reshape(blk_count, TOK_DEV, head_count)[block_perm]
    send_sum = sum_all.reshape(blk_count, TOK_DEV, head_count)[block_perm]
    recv_numer, recv_top, recv_sum = (
        lax.all_to_all(send_numer, "blk", split_axis=0, concat_axis=0, tiled=True),
        lax.all_to_all(send_top, "blk", split_axis=0, concat_axis=0, tiled=True),
        lax.all_to_all(send_sum, "blk", split_axis=0, concat_axis=0, tiled=True),
    )
    best_top = jnp.max(recv_top, axis=0)
    factor = jnp.exp(recv_top - best_top[None])
    total_sum = jnp.sum(recv_sum * factor, axis=0)
    total_numer = jnp.sum(
        recv_numer.reshape(blk_count, TOK_DEV, head_count, HD) * factor[..., None], axis=0
    )
    mixed = (total_numer / total_sum[:, :, None]).reshape(TOK_DEV, row_width).astype(jnp.bfloat16)
    head_term = jnp.dot(mixed, out_weight, preferred_element_type=jnp.float32)
    return lax.psum_scatter(head_term, "head", scatter_dimension=1, tiled=True).astype(jnp.bfloat16)


def solution(mesh):
    in_specs = (
        P("blk", "head"),
        P("blk", "head"),
        P("blk", "head"),
        P("blk", None, "head"),
        P("blk", None, "head"),
        P("head", None),
        P(),
        P(),
        P(),
    )
    out_specs = P("blk", "head")
    return jax.shard_map(shards, mesh=mesh, in_specs=in_specs, out_specs=out_specs, check_vma=False)
```

profile of v0, /device:TPU:10, one launch (start us, length us, event | category | flops | bytes accessed | tf_op | source)
XLA Modules:
  0.0 659.3 jit_solution(10038930395479542189)
XLA Ops:
  17.0 115.9 %all-gather.2.cloned.1.call-done = bf16[4096,448]{1,0:T(8,128)(2,1)} async-done(((bf16[64,448]{1,0:T(8,128)(2,1)}), bf16[4096,448]{1,0:T(8,128)(2,1)}) %all-gather.2.cloned.1.call-update) | async-done | bytes 3670032 | tf_op jit(solution)/shard_map/all_gather | solution.py:71
  132.9 5.0 gather_fusion.1
  137.9 6.2 copy.46
  144.1 2.4 constant_dynamic-slice_fusion.6
  146.4 2.2 copy.47
  148.7 3.9 broadcast_in_dim.152
  152.6 81.1 %while.18 = (s32[]{:T(128)}, f32[4,1024,2,224]{1,3,2,0:T(8,128)}, f32[4,1024,2]{1,2,0:T(2,128)S(1)}, f32[4,1024,2]{1,2,0:T(2,128)S(1)}, s32[8]{0:T(128)S(1)}, /*...) while((s32[]{:T(128)}, f32[4,1024,2,224]{1,3,2,0:T(8,128)}, ...), condition=%wide.region_5.6_spmd.clone, body=%wide.region_2.5_spmd.clone.sunk | while | flops 239149184 | bytes 14074583 | solution.py:104
  231.9 1.8 bitcast_dynamic-update-slice_fusion.10
  238.4 7.3 %all-to-all-start.2 = ((f32[64,1,128]{2,1,0:T(1,128)}), f32[64,1,128]{2,1,0:T(1,128)S(1)}, u32[]{:S(2)}, u32[]{:S(2)}) async-start(f32[64,1,128]{2,1,0:T(1,128)} %reshape.223), calls=%async_computation.2 | async-start | bytes 65536 | tf_op jit(solution)/shard_map/all_to_all | solution.py:121
  245.7 3.0 constant_dynamic-slice_fusion.7
  250.3 4.2 all-to-all-done.2
  254.6 6.4 all-to-all-start.1
  260.9 3.3 bitcast_dynamic-update-slice_fusion.3
  264.2 12.9 %copy.50 = f32[4,1024,2,224]{3,2,1,0:T(2,128)} copy(f32[4,1024,2,224]{1,3,2,0:T(8,128)} %bitcast_dynamic-update-slice_fusion.3) | data formatting | bytes 14680064 | tf_op jit(solution)/shard_map/jit(dynamic_update_index_in_dim)/dynamic_update_slice | solution.py:48
  277.1 11.7 %reshape.158 = f32[64,64,448]{2,1,0:T(8,128)} reshape(f32[4,1024,2,224]{3,2,1,0:T(2,128)} %copy.50) | data formatting | bytes 14680064 | tf_op jit(solution)/shard_map/reshape | solution.py:115
  288.8 7.8 %gather_fusion.2 = f32[64,64,448]{2,1,0:T(8,128)} fusion(f32[64,64,448]{2,1,0:T(8,128)} %reshape.158, s32[1024]{0:T(1024)} %copy-done.2), kind=kCustom, calls=%fused_computation.2 | custom fusion | bytes 14680320 | tf_op jit(solution)/shard_map/gather | solution.py:115
  296.7 10.8 %all-to-all-start = ((f32[64,64,448]{2,1,0:T(8,128)}), f32[64,64,448]{2,1,0:T(8,128)}, u32[]{:S(2)}, u32[]{:S(2)}) async-start(f32[64,64,448]{2,1,0:T(8,128)} %gather_fusion.2), calls=%async_computation | async-start | bytes 16777216 | tf_op jit(solution)/shard_map/all_to_all | solution.py:119
  310.4 2.0 copy.53
  312.5 6.9 %mul.121 = f32[64,64,2,224]{3,2,1,0:T(2,128)} broadcast(f32[64,64,2]{2,1,0:T(8,128)} %copy.53), dimensions={0,1,2} | broadcast | bytes 7372800 | tf_op jit(solution)/shard_map/mul | solution.py:127
  319.4 11.7 %mul.122 = f32[64,64,448]{2,1,0:T(8,128)} reshape(f32[64,64,2,224]{3,2,1,0:T(2,128)} %mul.121) | data formatting | bytes 14680064 | tf_op jit(solution)/shard_map/mul | solution.py:127
  331.1 186.4 %all-to-all-done = f32[64,64,448]{2,1,0:T(8,128)} async-done(((f32[64,64,448]{2,1,0:T(8,128)}), f32[64,64,448]{2,1,0:T(8,128)}, u32[]{:S(2)}, u32[]{:S(2)}) %all-to-all-start) | async-done | bytes 7340064 | tf_op jit(solution)/shard_map/all_to_all | solution.py:119
  517.5 7.7 %multiply_reduce_fusion = f32[64,448]{1,0:T(8,128)S(1)} fusion(f32[64,64,448]{2,1,0:T(8,128)} %all-to-all-done, f32[64,64,448]{2,1,0:T(8,128)} %mul.122), kind=kLoop, calls=%fused_computation.31 | loop fusion | flops 3641344 | bytes 14794752 | tf_op jit(solution)/shard_map/reduce_sum | solution.py:126
  525.2 2.8 convolution_bitcast_fusion
  528.0 122.8 %reduce-scatter.4.cloned.1.call-done = f32[448,64]{1,0:T(8,128)} async-done(((f32[3584,64]{1,0:T(8,128)}), f32[448,64]{1,0:T(8,128)}) %reduce-scatter.4.cloned.1.call-update) | async-done | bytes 114704
  (151 shorter events, 82.4 us)
Async XLA Ops:
  6.5 518.6 %copy-start = (bf16[448,3584]{1,0:T(8,128)(2,1)S(1)}, bf16[448,3584]{1,0:T(8,128)(2,1)}, u32[]{:S(2)}) copy-start(bf16[448,3584]{1,0:T(8,128)(2,1)} %param.16) | copy-start | bytes 9633796
  6.5 126.4 %all-gather.2.cloned.1.call-start = ((), (), s32[]{:S(2)}) async-start(), calls=%async_computation.4 | async-start | bytes 4259840 | tf_op jit(solution)/shard_map/all_gather | solution.py:71
  16.8 220.2 %copy-start.2 = (s32[1024]{0:T(1024)}, s32[1024]{0:T(1024)S(1)}, u32[]{:S(2)}) copy-start(s32[1024]{0:T(1024)S(1)} %pad_clamp_fusion) | copy-start | bytes 12292
  235.3 0.8 copy-start.1
  238.4 16.2 %all-to-all-start.2 = ((f32[64,1,128]{2,1,0:T(1,128)}), f32[64,1,128]{2,1,0:T(1,128)S(1)}, u32[]{:S(2)}, u32[]{:S(2)}) async-start(f32[64,1,128]{2,1,0:T(1,128)} %reshape.223), calls=%async_computation.2 | async-start | bytes 65536 | tf_op jit(solution)/shard_map/all_to_all | solution.py:121
  254.6 42.1 %all-to-all-start.1 = ((f32[64,1,128]{2,1,0:T(1,128)}), f32[64,1,128]{2,1,0:T(1,128)S(1)}, u32[]{:S(2)}, u32[]{:S(2)}) async-start(f32[64,1,128]{2,1,0:T(1,128)} %reshape.221), calls=%async_computation.1 | async-start | bytes 65536 | tf_op jit(solution)/shard_map/all_to_all | solution.py:120
  296.7 220.9 %all-to-all-start = ((f32[64,64,448]{2,1,0:T(8,128)}), f32[64,64,448]{2,1,0:T(8,128)}, u32[]{:S(2)}, u32[]{:S(2)}) async-start(f32[64,64,448]{2,1,0:T(8,128)} %gather_fusion.2), calls=%async_computation | async-start | bytes 16777216 | tf_op jit(solution)/shard_map/all_to_all | solution.py:119
  307.5 343.3 %reduce-scatter.4.cloned.1.call-start = ((), (), s32[]{:S(2)}) async-start(), calls=%async_computation.5 | async-start | bytes 2064384
Sparse Core Ops, SparseCore 0:
  9.5 123.3 all-gather.1
  528.1 122.6 reduce-scatter.3
where the time goes:
time: 662 us; the launch traced here: 659 us
  waiting for transfers between devices  430 us (65%)
  local copies, waits for them, and re-layouts  129 us (19%)
  starting transfers between devices  24.7 us (4%)
  matrix products  24.5 us (4%)
  other arithmetic  19 us (3%)
  between operations  16.1 us (2%)
  loops' own time  15.6 us (2%)
    all_to_all x1, waiting for transfers between devices, shards(): lax.all_to_all(send_numer, 'blk', split_axis=0, concat_axis=0, tiled=True)  186 us
    unnamed x3, waiting for transfers between devices  124 us
    all_gather x1, waiting for transfers between devices, shards(): gathered = lax.all_gather(queries, 'blk', axis=0, tiled=True)  116 us
    mul x2, local copies, waits for them, and re-layouts, shards(): recv_numer.reshape(blk_count, TOK_DEV, head_count, HD) * factor[..., None]  18.6 us
    dot_general x9, matrix products, block_partial(): jnp.einsum('hqk,khd->qhd', weights, value_heads, preferred_element_type=j...  17.2 us
    dynamic_slice x9, local copies, waits for them, and re-layouts, absorb(): old_numer = lax.dynamic_index_in_dim(numer_all, request, 0, keepdims=False)  16.6 us
    another operation x1, loops' own time, shards(): carry_state = lax.fori_loop(0, P_DEV, page_step, start_state)  15.6 us
  transfers between devices with their start and end apart: 5, of which 4 were waited for; matrix products, arithmetic and copies ran while one was open for 11% of the time, Pallas kernels for 0%

commit v1 on v0

v1 whole, which is shorter than its diff:
```python
import functools
import math

import jax
import jax.numpy as jnp
from jax import lax
from jax.experimental import pallas as pl
from jax.experimental.pallas import tpu as pltpu
from jax.sharding import PartitionSpec as P

HD = 224
PAGE = 128
P_DEV = 8
NEW = 1024
TOK_DEV = 64
MAXP = 128
REQS = 4
N_BLK = 64
BLK_PER_REQ = NEW // TOK_DEV
WIDE = 256
TQ = 512
QB = TQ // TOK_DEV
SLOTS = 2 * P_DEV + 2
POS = 24
LOG2_SCALE = math.log2(math.e) / math.sqrt(HD)
FLOOR = -1e20
MASKED = -1e30
K_ROWS = P_DEV * PAGE
PACK = 2 * K_ROWS + 2 * TOK_DEV


def attend(req, fill, off, inv, q_ref, own_ref, other_ref, out_ref, k_s, v_s, acc, top, pfill, poff, ends):
    lane = lax.broadcasted_iota(jnp.int32, (POS * PAGE, WIDE), 1)
    v_s[...] = jnp.where(lane >= HD, 1.0, 0.0).astype(jnp.bfloat16)
    for p in range(POS):
        pfill[p] = 0
        poff[p] = 0
    place = [jnp.int32(POS - 2)] * SLOTS
    pos = jnp.int32(0)
    for r in range(REQS):
        ends[2 * r] = pos // 2
        for i in range(SLOTS):
            hit = jnp.logical_and(req[i] == r, fill[i] > 0)
            place[i] = jnp.where(hit, pos, place[i])
            pos = pos + jnp.where(hit, 1, 0)
        pos = (pos + 1) // 2 * 2
        ends[2 * r + 1] = pos // 2
    for i in range(SLOTS):
        pfill[place[i]] = fill[i]
        poff[place[i]] = off[i]
        if i < 2 * P_DEV:
            src = own_ref if i < P_DEV else other_ref
            row = (i % P_DEV) * PAGE
            dst = pl.ds(pl.multiple_of(place[i] * PAGE, PAGE), PAGE)
            k_s[dst, :] = src[row : row + PAGE, :]
            v_s[dst, :HD] = src[K_ROWS + row : K_ROWS + row + PAGE, :]
        else:
            src = own_ref if i == 2 * P_DEV else other_ref
            row = 2 * K_ROWS
            dst = pl.ds(pl.multiple_of(place[i] * PAGE, PAGE), TOK_DEV)
            k_s[dst, :] = src[row : row + TOK_DEV, :]
            v_s[dst, :HD] = src[row + TOK_DEV : row + 2 * TOK_DEV, :]

    key_id = lax.broadcasted_iota(jnp.int32, (TQ, PAGE), 1)
    row_id = lax.broadcasted_iota(jnp.int32, (TQ, PAGE), 0)
    out_lane = lax.broadcasted_iota(jnp.int32, (TQ, WIDE), 1)

    def tile(step, _):
        r = step // (NEW // TQ)
        t = step % (NEW // TQ)
        first = step * QB
        q = jnp.concatenate([q_ref[inv[first + u]] for u in range(QB)], axis=0)
        acc[...] = jnp.zeros((TQ, WIDE), jnp.float32)
        top[...] = jnp.full((TQ, PAGE), FLOOR, jnp.float32)
        row_pos = row_id + t * TQ

        def chunk(c, _):
            at = pl.ds(pl.multiple_of(c * 2 * PAGE, 2 * PAGE), 2 * PAGE)
            s = lax.dot_general(q, k_s[at, :], (((1,), (1,)), ((), ())), preferred_element_type=jnp.float32)
            parts = []
            for half in range(2):
                limit = jnp.minimum(row_pos - poff[2 * c + half], pfill[2 * c + half] - 1)
                s_half = s[:, half * PAGE : (half + 1) * PAGE] * LOG2_SCALE
                parts.append(jnp.where(key_id <= limit, s_half, MASKED))
            old = top[...]
            best = jnp.max(jnp.maximum(parts[0], parts[1]), axis=1, keepdims=True)
            new = jnp.maximum(old, best)
            w = jnp.concatenate([jnp.exp2(x - new).astype(jnp.bfloat16) for x in parts], axis=1)
            factor = jnp.exp2(old - new)
            part = jnp.dot(w, v_s[at, :], preferred_element_type=jnp.float32)
            acc[:, :PAGE] = acc[:, :PAGE] * factor + part[:, :PAGE]
            acc[:, PAGE:] = acc[:, PAGE:] * factor + part[:, PAGE:]
            top[...] = new
            return 0

        lax.fori_loop(ends[2 * r], ends[2 * r + 1], chunk, 0)
        old = top[...]
        up = old + jnp.abs(old) * (2.0**-15)
        high = up.astype(jnp.bfloat16).astype(jnp.float32)
        low = (up - high).astype(jnp.bfloat16).astype(jnp.float32)
        factor = jnp.exp2(old - (high + low))
        left = acc[:, :PAGE] * factor
        right = acc[:, PAGE:] * factor
        total = jnp.broadcast_to(right[:, HD - PAGE : HD - PAGE + 1], (TQ, PAGE))
        total_low = total - total.astype(jnp.bfloat16).astype(jnp.float32)
        tail = key_id + PAGE
        right = jnp.where(tail == HD + 1, high, right)
        right = jnp.where(tail == HD + 2, low, right)
        right = jnp.where(tail == HD + 3, total_low, right)
        result = jnp.concatenate([left.astype(jnp.bfloat16), right.astype(jnp.bfloat16)], axis=1)
        for u in range(QB):
            out_ref[inv[first + u]] = result[u * TOK_DEV : (u + 1) * TOK_DEV]
        return 0

    lax.fori_loop(0, REQS * NEW // TQ, tile, 0)


def merge_project(x_ref, w_ref, out_ref, mixed):
    n_src = N_BLK // 2
    for h in range(2):

        def top_of(s, best):
            x = x_ref[2 * s + h, :, PAGE:].astype(jnp.float32)
            return jnp.maximum(best, x[:, HD + 1 - PAGE : HD + 2 - PAGE] + x[:, HD + 2 - PAGE : HD + 3 - PAGE])

        best = lax.fori_loop(0, n_src, top_of, jnp.full((TOK_DEV, 1), MASKED, jnp.float32), unroll=4)

        def add(s, total):
            x = x_ref[2 * s + h].astype(jnp.float32)
            here = x[:, HD + 1 : HD + 2] + x[:, HD + 2 : HD + 3]
            return total + x * jnp.exp2(here - best)

        total = lax.fori_loop(0, n_src, add, jnp.zeros((TOK_DEV, WIDE), jnp.float32), unroll=4)
        mass = total[:, HD : HD + 1] + total[:, HD + 3 : HD + 4]
        mixed[:, h * HD : (h + 1) * HD] = (total[:, :HD] / mass).astype(jnp.bfloat16)
    y = jnp.dot(mixed[...], w_ref[...], preferred_element_type=jnp.float32)
    width = out_ref.shape[2]
    for h in range(out_ref.shape[0]):
        out_ref[h] = y[:, h * width : (h + 1) * width].astype(jnp.bfloat16)


def shards(queries, new_keys, new_values, key_cache, value_cache, out_weight, cache_len, page_table, block_perm):
    row_width = queries.shape[1]
    me = lax.axis_index("blk")
    core = me % 2
    partner = me + 1 - 2 * core

    def half(x, which):
        return jnp.where(which == 0, x[:, :HD], x[:, HD:])

    packed = jnp.concatenate(
        [key_cache.reshape(K_ROWS, row_width), value_cache.reshape(K_ROWS, row_width), new_keys, new_values], axis=0
    )
    own = half(packed, core)
    send = half(packed, 1 - core)
    other = lax.ppermute(send, "blk", [(d, d ^ 1) for d in range(N_BLK)])

    spread = jnp.broadcast_to(
        jnp.stack([queries[:, :HD], queries[:, HD:]])[None], (N_BLK // 2, 2, TOK_DEV, HD)
    ).reshape(N_BLK, TOK_DEV, HD)
    query_all = lax.all_to_all(spread, "blk", split_axis=0, concat_axis=0, tiled=True)

    page_ids = jnp.concatenate([me * P_DEV + jnp.arange(P_DEV), partner * P_DEV + jnp.arange(P_DEV)])
    table_ids = jnp.arange(page_table.shape[0], dtype=jnp.int32)
    logical = jnp.sum(jnp.where(page_table[None, :] == page_ids[:, None], table_ids[None, :], 0), axis=1)
    page_req = logical // MAXP
    req_ids = jnp.arange(REQS, dtype=jnp.int32)
    page_len = jnp.sum(jnp.where(page_req[:, None] == req_ids[None, :], cache_len[None, :], 0), axis=1)
    page_fill = jnp.clip(page_len - logical % MAXP * PAGE, 0, PAGE)
    block_ids = jnp.arange(N_BLK, dtype=jnp.int32)
    mine = jnp.stack([me, partner])
    new_block = jnp.sum(jnp.where(block_ids[None, :] == mine[:, None], block_perm[None, :], 0), axis=1)
    inverse = jnp.sum(jnp.where(block_perm[None, :] == block_ids[:, None], block_ids[None, :], 0), axis=1)
    req = jnp.concatenate([page_req, new_block // BLK_PER_REQ]).astype(jnp.int32)
    fill = jnp.concatenate([page_fill, jnp.full((2,), TOK_DEV, jnp.int32)]).astype(jnp.int32)
    off = jnp.concatenate(
        [jnp.full((2 * P_DEV,), -(2**20), jnp.int32), new_block % BLK_PER_REQ * TOK_DEV]
    ).astype(jnp.int32)

    whole = pl.BlockSpec(memory_space=pltpu.VMEM)
    partial = pl.pallas_call(
        attend,
        out_shape=jax.ShapeDtypeStruct((N_BLK, TOK_DEV, WIDE), jnp.bfloat16),
        in_specs=[pl.BlockSpec(memory_space=pltpu.SMEM)] * 4 + [whole] * 3,
        out_specs=whole,
        scratch_shapes=[
            pltpu.VMEM((POS * PAGE, HD), jnp.bfloat16),
            pltpu.VMEM((POS * PAGE, WIDE), jnp.bfloat16),
            pltpu.VMEM((TQ, WIDE), jnp.float32),
            pltpu.VMEM((TQ, PAGE), jnp.float32),
            pltpu.SMEM((POS,), jnp.int32),
            pltpu.SMEM((POS,), jnp.int32),
            pltpu.SMEM((2 * REQS,), jnp.int32),
        ],
        name="attend",
    )(req, fill, off, inverse.astype(jnp.int32), query_all, own, other)

    gathered = lax.all_to_all(partial, "blk", split_axis=0, concat_axis=0, tiled=True)
    n_head = lax.axis_size("head")
    terms = pl.pallas_call(
        merge_project,
        out_shape=jax.ShapeDtypeStruct((n_head, TOK_DEV, row_width), jnp.bfloat16),
        in_specs=[whole, whole],
        out_specs=whole,
        scratch_shapes=[pltpu.VMEM((TOK_DEV, row_width), jnp.bfloat16)],
        name="merge_project",
    )(gathered, out_weight)
    terms = lax.all_to_all(terms, "head", split_axis=0, concat_axis=0, tiled=True)
    return jnp.sum(terms.astype(jnp.float32), axis=0).astype(jnp.bfloat16)


def solution(mesh):
    in_specs = (
        P("blk", "head"),
        P("blk", "head"),
        P("blk", "head"),
        P("blk", None, "head"),
        P("blk", None, "head"),
        P("head", None),
        P(),
        P(),
        P(),
    )
    return jax.shard_map(shards, mesh=mesh, in_specs=in_specs, out_specs=P("blk", "head"), check_vma=False)
```

time: 662 us -> 180 us (0.27)
  the two profiles are of different devices: /device:TPU:10 before, /device:TPU:9 now
where the time goes in v1:
time: 180 us; the launch traced here: 179 us
  blocking collectives  83.9 us (47%)
  waiting for transfers between devices  36.3 us (20%)
  Pallas kernels  24.6 us (14%)
  starting transfers between devices  16.9 us (9%)
  local copies, waits for them, and re-layouts  11.7 us (6%)
  other arithmetic  5.55 us (3%)
    all_to_all x1, blocking collectives, shards(): lax.all_to_all(partial, 'blk', split_axis=0, concat_axis=0, tiled=True)  57.4 us
    all_to_all x1, waiting for transfers between devices, shards(): lax.all_to_all(spread, 'blk', split_axis=0, concat_axis=0, tiled=True)  36.3 us
    all_to_all x1, blocking collectives, shards(): lax.all_to_all(terms, 'head', split_axis=0, concat_axis=0, tiled=True)  26.5 us
    pallas_call x1, Pallas kernels, shards(): pl.pallas_call(attend, out_shape=jax.ShapeDtypeStruct((N_BLK, TOK_DEV, WI...  15.8 us
    all_to_all x1, starting transfers between devices, shards(): lax.all_to_all(spread, 'blk', split_axis=0, concat_axis=0, tiled=True)  14.6 us
    pallas_call x1, Pallas kernels, shards(): pl.pallas_call(merge_project, out_shape=jax.ShapeDtypeStruct((n_head, TOK...  8.8 us
    unnamed x14, local copies, waits for them, and re-layouts  5.08 us
  transfers between devices with their start and end apart: 2, of which 1 were waited for; matrix products, arithmetic and copies ran while one was open for 7% of the time, Pallas kernels for 0%

profile of v1, /device:TPU:9, one launch (start us, length us, event | category | flops | bytes accessed | tf_op | source)
XLA Modules:
  0.0 179.1 jit_solution(3036863344809706625)
XLA Ops:
  0.0 1.0 slice_bitcast_fusion.1
  1.0 1.6 broadcast_in_dim.74
  2.6 14.6 %all-to-all-start = ((bf16[64,64,224]{2,1,0:T(8,128)(2,1)}), bf16[64,64,224]{2,1,0:T(8,128)(2,1)S(1)}, u32[]{:S(2)}, u32[]{:S(2)}) async-start(bf16[64,64,224]{2,1,0:T(8,128)(2,1)} %bitcast.9), calls=%async_computation | async-start | bytes 4194304 | tf_op jit(solution)/shard_map/all_to_all | solution.py:161
  17.3 1.5 copy.16
  18.8 2.3 %copy.17 = bf16[8,128,448]{2,1,0:T(8,128)(2,1)} copy(bf16[8,128,448]{1,2,0:T(8,128)(2,1)} %param.13) | data formatting | bytes 1835008 | tf_op args[4]
  21.0 1.5 pad_maximum_fusion
  22.6 1.4 broadcast_select_fusion
  24.0 1.5 copy.18
  25.5 2.3 %collective-permute-start = (bf16[2176,224]{0,1:T(8,128)(2,1)}, bf16[2176,224]{0,1:T(8,128)(2,1)S(1)}, u32[]{:S(2)}, u32[]{:S(2)}) collective-permute-start(bf16[2176,224]{0,1:T(8,128)(2,1)} %copy.18), channel_id=1, source_target_pairs={{0,8},{8,0},{16,24},{24,16},{32,40},{40,32},{48,56},{56,48},{64,72... | collective-permute-start | bytes 2924552 | tf_op jit(solution)/shard_map/ppermute | solution.py:156
  27.9 0.2 select_reduce_fusion.1
  28.1 0.1 select_reduce_fusion.2
  28.2 0.5 concatenate.17.fill
  28.8 0.2 fusion
  29.0 0.6 concatenate.18.off
  29.6 0.6 pad_add_fusion.2.req
  30.1 0.6 select_reduce_fusion.inv
  30.8 1.5 copy.19.other_ref
  32.3 36.3 %all-to-all-done.q_ref = bf16[64,64,224]{2,1,0:T(8,128)(2,1)S(1)} async-done(((bf16[64,64,224]{2,1,0:T(8,128)(2,1)}), bf16[64,64,224]{2,1,0:T(8,128)(2,1)S(1)}, u32[]{:S(2)}, u32[]{:S(2)}) %all-to-all-start) | async-done | bytes 1835040 | tf_op jit(solution)/shard_map/all_to_all | solution.py:161
  68.6 1.3 copy-done
  69.9 15.8 %attend.1 = bf16[64,64,256]{2,1,0:T(8,128)(2,1)} custom-call(s32[18]{0:T(128)} %pad_add_fusion.2.req, s32[18]{0:T(128)} %concatenate.17.fill, s32[18]{0:T(128)} %concatenate.18.off, s32[64]{0:T(128)} %select_reduce_fusion.inv, bf16[64,64,224]{2,1,0:T(8,128)(2,1)} %copy-done, bf16[2176,224]{1,0:T(8,128)(2,1)} %get-tuple-element.6.own_ref, ...), custom_call_target="tpu_custom_call" | custom-call | tf_op jit(solution)/shard_map/attend/pallas_call | solution.py:181
  85.7 57.4 %all_to_all.15.x_ref = bf16[64,64,256]{2,1,0:T(8,128)(2,1)} all-to-all(bf16[64,64,256]{2,1,0:T(8,128)(2,1)} %attend.1), channel_id=1, replica_groups=mesh['blk'=64,'head'=8] {'blk'}, dimensions={0} | all-to-all | bytes 4194304 | tf_op jit(solution)/shard_map/all_to_all | solution.py:198
  143.1 8.8 %merge_project.1 = bf16[8,64,448]{2,1,0:T(8,128)(2,1)} custom-call(bf16[64,64,256]{2,1,0:T(8,128)(2,1)} %all_to_all.15.x_ref, bf16[448,3584]{1,0:T(8,128)(2,1)} %w_ref.1), custom_call_target="tpu_custom_call" | custom-call | tf_op jit(solution)/shard_map/merge_project/pallas_call | solution.py:200
  151.9 26.5 %all_to_all.16 = bf16[8,64,448]{2,1,0:T(8,128)(2,1)S(1)} all-to-all(bf16[8,64,448]{2,1,0:T(8,128)(2,1)} %merge_project.1), channel_id=1, replica_groups=mesh['blk'=64,'head'=8] {'head'}, dimensions={0} | all-to-all | bytes 917504 | tf_op jit(solution)/shard_map/all_to_all | solution.py:208
  178.4 0.7 reduce_sum.52
  (19 shorter events, 0.2 us)
Async XLA Ops:
  2.6 66.1 %all-to-all-start = ((bf16[64,64,224]{2,1,0:T(8,128)(2,1)}), bf16[64,64,224]{2,1,0:T(8,128)(2,1)S(1)}, u32[]{:S(2)}, u32[]{:S(2)}) async-start(bf16[64,64,224]{2,1,0:T(8,128)(2,1)} %bitcast.9), calls=%async_computation | async-start | bytes 4194304 | tf_op jit(solution)/shard_map/all_to_all | solution.py:161
  17.2 3.8 %copy-start.1 = (bf16[64,448]{1,0:T(8,128)(2,1)S(1)}, bf16[64,448]{1,0:T(8,128)(2,1)}, u32[]{:S(2)}) copy-start(bf16[64,448]{1,0:T(8,128)(2,1)} %param.11) | copy-start | bytes 172036
  17.2 3.8 %copy-start.2 = (bf16[64,448]{1,0:T(8,128)(2,1)S(1)}, bf16[64,448]{1,0:T(8,128)(2,1)}, u32[]{:S(2)}) copy-start(bf16[64,448]{1,0:T(8,128)(2,1)} %param.10) | copy-start | bytes 172036
  22.6 5.3 %copy-start.3 = (s32[512]{0:T(512)S(1)}, s32[512]{0:T(512)}, u32[]{:S(2)}) copy-start(s32[512]{0:T(512)} %param.16) | copy-start | bytes 6148
  22.6 5.5 %copy-start.4 = (s32[4]{0:T(128)S(1)}, s32[4]{0:T(128)}, u32[]{:S(2)}) copy-start(s32[4]{0:T(128)} %param.15) | copy-start | bytes 52
  22.6 6.2 %copy-start.5 = (s32[64]{0:T(128)S(1)}, s32[64]{0:T(128)}, u32[]{:S(2)}) copy-start(s32[64]{0:T(128)} %param.17) | copy-start | bytes 772
  25.5 5.3 %collective-permute-start = (bf16[2176,224]{0,1:T(8,128)(2,1)}, bf16[2176,224]{0,1:T(8,128)(2,1)S(1)}, u32[]{:S(2)}, u32[]{:S(2)}) collective-permute-start(bf16[2176,224]{0,1:T(8,128)(2,1)} %copy.18), channel_id=1, source_target_pairs={{0,8},{8,0},{16,24},{24,16},{32,40},{40,32},{48,56},{56,48},{64,72... | collective-permute-start | bytes 2924552 | tf_op jit(solution)/shard_map/ppermute | solution.py:156
  68.6 1.3 copy-start

commit v2 on v1

--- a/solution.py
+++ b/solution.py
@@ -25,11 +25,17 @@
 LOG2_SCALE = math.log2(math.e) / math.sqrt(HD)
 FLOOR = -1e20
 MASKED = -1e30
+LIMIT = 40 << 20
 K_ROWS = P_DEV * PAGE
+CHIPS = N_BLK // 2
+CHIP_ROWS = 2 * TOK_DEV
+TAIL = HD - PAGE
+STEP = PAGE - TAIL
+Q_PACK = CHIP_ROWS * HD // PAGE
 PACK = 2 * K_ROWS + 2 * TOK_DEV
 
 
-def attend(req, fill, off, inv, q_ref, own_ref, other_ref, out_ref, k_s, v_s, acc, top, pfill, poff, ends):
+def attend(req, fill, off, inv, q_ref, own_ref, other_ref, out_ref, k_s, v_s, q_s, acc, top, pfill, poff, ends):
     lane = lax.broadcasted_iota(jnp.int32, (POS * PAGE, WIDE), 1)
     v_s[...] = jnp.where(lane >= HD, 1.0, 0.0).astype(jnp.bfloat16)
     for p in range(POS):
@@ -61,6 +67,18 @@
             k_s[dst, :] = src[row : row + TOK_DEV, :]
             v_s[dst, :HD] = src[row + TOK_DEV : row + 2 * TOK_DEV, :]
 
+    def unfold(i, _):
+        for b in range(2):
+            q_s[2 * i + b, :, :PAGE] = q_ref[i, b * TOK_DEV : (b + 1) * TOK_DEV, :]
+        q_s[2 * i, :, PAGE:] = q_ref[i, PAGE : PAGE + TOK_DEV, :TAIL]
+        q_s[2 * i + 1, :STEP, PAGE:] = q_ref[i, PAGE + TOK_DEV : PAGE + TAIL, :TAIL]
+        q_s[2 * i + 1, STEP:, PAGE:] = jnp.concatenate(
+            [q_ref[i, PAGE + k * STEP : PAGE + (k + 1) * STEP, TAIL:] for k in range(TAIL // STEP)], axis=1
+        )
+        return 0
+
+    lax.fori_loop(0, CHIPS, unfold, 0, unroll=2)
+
     key_id = lax.broadcasted_iota(jnp.int32, (TQ, PAGE), 1)
     row_id = lax.broadcasted_iota(jnp.int32, (TQ, PAGE), 0)
     out_lane = lax.broadcasted_iota(jnp.int32, (TQ, WIDE), 1)
@@ -69,7 +87,7 @@
         r = step // (NEW // TQ)
         t = step % (NEW // TQ)
         first = step * QB
-        q = jnp.concatenate([q_ref[inv[first + u]] for u in range(QB)], axis=0)
+        q = jnp.concatenate([q_s[inv[first + u]] for u in range(QB)], axis=0)
         acc[...] = jnp.zeros((TQ, WIDE), jnp.float32)
         top[...] = jnp.full((TQ, PAGE), FLOOR, jnp.float32)
         row_pos = row_id + t * TQ
@@ -115,28 +133,59 @@
     lax.fori_loop(0, REQS * NEW // TQ, tile, 0)
 
 
-def merge_project(x_ref, w_ref, out_ref, mixed):
-    n_src = N_BLK // 2
-    for h in range(2):
-
-        def top_of(s, best):
-            x = x_ref[2 * s + h, :, PAGE:].astype(jnp.float32)
-            return jnp.maximum(best, x[:, HD + 1 - PAGE : HD + 2 - PAGE] + x[:, HD + 2 - PAGE : HD + 3 - PAGE])
-
-        best = lax.fori_loop(0, n_src, top_of, jnp.full((TOK_DEV, 1), MASKED, jnp.float32), unroll=4)
-
-        def add(s, total):
-            x = x_ref[2 * s + h].astype(jnp.float32)
-            here = x[:, HD + 1 : HD + 2] + x[:, HD + 2 : HD + 3]
-            return total + x * jnp.exp2(here - best)
-
-        total = lax.fori_loop(0, n_src, add, jnp.zeros((TOK_DEV, WIDE), jnp.float32), unroll=4)
-        mass = total[:, HD : HD + 1] + total[:, HD + 3 : HD + 4]
-        mixed[:, h * HD : (h + 1) * HD] = (total[:, :HD] / mass).astype(jnp.bfloat16)
-    y = jnp.dot(mixed[...], w_ref[...], preferred_element_type=jnp.float32)
+def fold_queries(core, own_ref, other_ref, out_ref, chip):
+    mine = pl.ds(pl.multiple_of(core[0] * TOK_DEV, TOK_DEV), TOK_DEV)
+    theirs = pl.ds(pl.multiple_of((1 - core[0]) * TOK_DEV, TOK_DEV), TOK_DEV)
+    chip[mine, :] = own_ref[...]
+    chip[theirs, :] = other_ref[...]
+    rows = chip[...]
+    tail = rows[:, PAGE:]
+    folded = jnp.concatenate([tail[TAIL:, k * STEP : (k + 1) * STEP] for k in range(TAIL // STEP)], axis=0)
+    pack = jnp.concatenate([rows[:, :PAGE], jnp.concatenate([tail[:TAIL], folded], axis=1)], axis=0)
+    out_ref[...] = jnp.broadcast_to(pack[None], (CHIPS, Q_PACK, PAGE))
+
+
+def merge(core, x_ref, mine_ref, theirs_ref, tops, acc, rows):
+    def top_of(s, best):
+        x = x_ref[s, :, PAGE:].astype(jnp.float32)
+        here = x[:, TAIL + 1 : TAIL + 2] + x[:, TAIL + 2 : TAIL + 3]
+        here = jnp.broadcast_to(here, (CHIP_ROWS, PAGE))
+        tops[s] = here
+        return jnp.maximum(best, here)
+
+    best = lax.fori_loop(0, CHIPS, top_of, jnp.full((CHIP_ROWS, PAGE), MASKED, jnp.float32), unroll=4)
+    acc[...] = jnp.zeros((CHIP_ROWS, WIDE), jnp.float32)
+
+    def add(g, _):
+        for part in range(2):
+            lanes = slice(part * PAGE, (part + 1) * PAGE)
+            total = acc[:, lanes]
+            for u in range(4):
+                factor = jnp.exp2(tops[4 * g + u] - best)
+                total = total + x_ref[4 * g + u, :, lanes].astype(jnp.float32) * factor
+            acc[:, lanes] = total
+        return 0
+
+    lax.fori_loop(0, CHIPS // 4, add, 0)
+    total = acc[...]
+    mass = total[:, HD : HD + 1] + total[:, HD + 3 : HD + 4]
+    rows[...] = (total[:, :HD] / mass).astype(jnp.bfloat16)
+    mine_ref[...] = rows[pl.ds(pl.multiple_of(core[0] * TOK_DEV, TOK_DEV), TOK_DEV), :]
+    theirs_ref[...] = rows[pl.ds(pl.multiple_of((1 - core[0]) * TOK_DEV, TOK_DEV), TOK_DEV), :]
+
+
+def project(core, mine_ref, other_ref, w_ref, out_ref):
+    mine_rows = pl.ds(pl.multiple_of(core[0] * HD, HD), HD)
+    other_rows = pl.ds(pl.multiple_of((1 - core[0]) * HD, HD), HD)
+    y = jnp.dot(mine_ref[...], w_ref[mine_rows, :], preferred_element_type=jnp.float32)
+    y = y + jnp.dot(other_ref[...], w_ref[other_rows, :], preferred_element_type=jnp.float32)
     width = out_ref.shape[2]
     for h in range(out_ref.shape[0]):
         out_ref[h] = y[:, h * width : (h + 1) * width].astype(jnp.bfloat16)
+
+
+def in_vmem(x):
+    return pltpu.with_memory_space_constraint(x, pltpu.VMEM)
 
 
 def shards(queries, new_keys, new_values, key_cache, value_cache, out_weight, cache_len, page_table, block_perm):
@@ -155,10 +204,25 @@
     send = half(packed, 1 - core)
     other = lax.ppermute(send, "blk", [(d, d ^ 1) for d in range(N_BLK)])
 
-    spread = jnp.broadcast_to(
-        jnp.stack([queries[:, :HD], queries[:, HD:]])[None], (N_BLK // 2, 2, TOK_DEV, HD)
-    ).reshape(N_BLK, TOK_DEV, HD)
-    query_all = lax.all_to_all(spread, "blk", split_axis=0, concat_axis=0, tiled=True)
+    swap = [(d, d ^ 1) for d in range(N_BLK)]
+    groups = [[2 * i + c for i in range(CHIPS)] for c in range(2)]
+    q_own = half(queries, core)
+    q_other = lax.ppermute(half(queries, 1 - core), "blk", swap)
+    whole = pl.BlockSpec(memory_space=pltpu.VMEM)
+    scalar = pl.BlockSpec(memory_space=pltpu.SMEM)
+    core_id = core.reshape(1).astype(jnp.int32)
+    spread = pl.pallas_call(
+        fold_queries,
+        out_shape=pltpu.VMEM((CHIPS, Q_PACK, PAGE), jnp.bfloat16),
+        in_specs=[scalar, whole, whole],
+        out_specs=whole,
+        scratch_shapes=[pltpu.VMEM((CHIP_ROWS, HD), jnp.bfloat16)],
+        compiler_params=pltpu.CompilerParams(vmem_limit_bytes=LIMIT),
+        name="fold_queries",
+    )(core_id, q_own, q_other)
+    query_all = lax.all_to_all(
+        spread, "blk", split_axis=0, concat_axis=0, tiled=True, axis_index_groups=groups
+    )
 
     page_ids = jnp.concatenate([me * P_DEV + jnp.arange(P_DEV), partner * P_DEV + jnp.arange(P_DEV)])
     table_ids = jnp.arange(page_table.shape[0], dtype=jnp.int32)
@@ -177,34 +241,56 @@
         [jnp.full((2 * P_DEV,), -(2**20), jnp.int32), new_block % BLK_PER_REQ * TOK_DEV]
     ).astype(jnp.int32)
 
-    whole = pl.BlockSpec(memory_space=pltpu.VMEM)
     partial = pl.pallas_call(
         attend,
-        out_shape=jax.ShapeDtypeStruct((N_BLK, TOK_DEV, WIDE), jnp.bfloat16),
+        out_shape=pltpu.VMEM((N_BLK, TOK_DEV, WIDE), jnp.bfloat16),
         in_specs=[pl.BlockSpec(memory_space=pltpu.SMEM)] * 4 + [whole] * 3,
         out_specs=whole,
         scratch_shapes=[
             pltpu.VMEM((POS * PAGE, HD), jnp.bfloat16),
             pltpu.VMEM((POS * PAGE, WIDE), jnp.bfloat16),
+            pltpu.VMEM((N_BLK, TOK_DEV, HD), jnp.bfloat16),
             pltpu.VMEM((TQ, WIDE), jnp.float32),
             pltpu.VMEM((TQ, PAGE), jnp.float32),
             pltpu.SMEM((POS,), jnp.int32),
             pltpu.SMEM((POS,), jnp.int32),
             pltpu.SMEM((2 * REQS,), jnp.int32),
         ],
+        compiler_params=pltpu.CompilerParams(vmem_limit_bytes=LIMIT),
         name="attend",
-    )(req, fill, off, inverse.astype(jnp.int32), query_all, own, other)
-
-    gathered = lax.all_to_all(partial, "blk", split_axis=0, concat_axis=0, tiled=True)
+    )(req, fill, off, inverse.astype(jnp.int32), in_vmem(query_all), own, other)
+
+    gathered = lax.all_to_all(
+        partial.reshape(CHIPS, CHIP_ROWS, WIDE),
+        "blk",
+        split_axis=0,
+        concat_axis=0,
+        tiled=True,
+        axis_index_groups=groups,
+    )
     n_head = lax.axis_size("head")
+    mine_rows, their_rows = pl.pallas_call(
+        merge,
+        out_shape=[jax.ShapeDtypeStruct((TOK_DEV, HD), jnp.bfloat16)] * 2,
+        in_specs=[scalar, whole],
+        out_specs=[whole, whole],
+        scratch_shapes=[
+            pltpu.VMEM((CHIPS, CHIP_ROWS, PAGE), jnp.float32),
+            pltpu.VMEM((CHIP_ROWS, WIDE), jnp.float32),
+            pltpu.VMEM((CHIP_ROWS, HD), jnp.bfloat16),
+        ],
+        compiler_params=pltpu.CompilerParams(vmem_limit_bytes=LIMIT),
+        name="merge",
+    )(core_id, in_vmem(gathered))
+    other_rows = lax.ppermute(their_rows, "blk", swap)
     terms = pl.pallas_call(
-        merge_project,
-        out_shape=jax.ShapeDtypeStruct((n_head, TOK_DEV, row_width), jnp.bfloat16),
-        in_specs=[whole, whole],
+        project,
+        out_shape=pltpu.VMEM((n_head, TOK_DEV, row_width), jnp.bfloat16),
+        in_specs=[scalar, whole, whole, whole],
         out_specs=whole,
-        scratch_shapes=[pltpu.VMEM((TOK_DEV, row_width), jnp.bfloat16)],
-        name="merge_project",
-    )(gathered, out_weight)
+        compiler_params=pltpu.CompilerParams(vmem_limit_bytes=LIMIT),
+        name="project",
+    )(core_id, mine_rows, other_rows, out_weight)
     terms = lax.all_to_all(terms, "head", split_axis=0, concat_axis=0, tiled=True)
     return jnp.sum(terms.astype(jnp.float32), axis=0).astype(jnp.bfloat16)
 

time: 180 us -> 171 us (0.950)
  starting transfers between devices: 16.9 us -> 23.8 us
  Pallas kernels: 24.6 us -> 19 us
  waiting for transfers between devices: 36.3 us -> 31 us
  blocking collectives: 83.9 us -> 80.9 us
    all_to_all x1, waiting for transfers between devices: 36.3 us -> 27.8 us  [shards(): lax.all_to_all(spread, 'blk', split_axis=0, concat_axis=0, tiled=True, ax...]
    ppermute x0 -> x2, starting transfers between devices: none -> 7.59 us  [the longest x1 5.01 us: shards(): other_rows = lax.ppermute(their_rows, 'blk', swap)]
    pallas_call x2 -> x4, Pallas kernels: 24.6 us -> 19 us  [the longest x1 15.2 us: shards(): pl.pallas_call(attend, out_shape=pltpu.VMEM((N_BLK, TOK_DEV, WIDE), jnp.b...]
    all_to_all x1, blocking collectives: 57.4 us -> 54.5 us  [shards(): lax.all_to_all(partial.reshape(CHIPS, CHIP_ROWS, WIDE), 'blk', split_axis...]
    unnamed x14 -> x18, local copies, waits for them, and re-layouts: 5.08 us -> 6.29 us
  transfers between devices with their start and end apart: 2 -> 4, of which waited for: 1 -> 4; matrix products, arithmetic and copies ran while one was open for 7% -> 7% of each run, Pallas kernels for 0% -> 0%
where the time goes in v2:
time: 171 us
  blocking collectives  80.9 us (47%)
  waiting for transfers between devices  31 us (18%)
  starting transfers between devices  23.8 us (14%)
  Pallas kernels  19 us (11%)
  local copies, waits for them, and re-layouts  11.1 us (6%)
  other arithmetic  5.44 us (3%)
    all_to_all x1, blocking collectives, shards(): lax.all_to_all(partial.reshape(CHIPS, CHIP_ROWS, WIDE), 'blk', split_axis...  54.5 us
    all_to_all x1, waiting for transfers between devices, shards(): lax.all_to_all(spread, 'blk', split_axis=0, concat_axis=0, tiled=True, ax...  27.8 us
    all_to_all x1, blocking collectives, shards(): lax.all_to_all(terms, 'head', split_axis=0, concat_axis=0, tiled=True)  26.4 us
    pallas_call x1, Pallas kernels, shards(): pl.pallas_call(attend, out_shape=pltpu.VMEM((N_BLK, TOK_DEV, WIDE), jnp.b...  15.2 us
    all_to_all x1, starting transfers between devices, shards(): lax.all_to_all(spread, 'blk', split_axis=0, concat_axis=0, tiled=True, ax...  13.4 us
    unnamed x18, local copies, waits for them, and re-layouts  6.29 us
    ppermute x1, starting transfers between devices, shards(): other_rows = lax.ppermute(their_rows, 'blk', swap)  5.01 us
  transfers between devices with their start and end apart: 4, of which 4 were waited for; matrix products, arithmetic and copies ran while one was open for 7% of the time, Pallas kernels for 0%

profile of v2, /device:TPU:9, one launch (start us, length us, event | category | flops | bytes accessed | tf_op | source)
XLA Modules:
  0.0 171.4 jit_solution(9591238159080009828)
XLA Ops:
  0.0 1.0 broadcast_select_fusion.2
  1.0 2.6 %collective-permute-start = (bf16[64,224]{1,0:T(8,128)(2,1)S(1)}, bf16[64,224]{1,0:T(8,128)(2,1)S(1)}, u32[]{:S(2)}, u32[]{:S(2)}) collective-permute-start(bf16[64,224]{1,0:T(8,128)(2,1)S(1)} %get-tuple-element.11), channel_id=1, source_target_pairs={{0,8},{8,0},{16,24},{24,16},{32,40},{40,32},{48,56},{56,48},{64,72... | collective-permute-start | bytes 86024 | tf_op jit(solution)/shard_map/ppermute | solution.py:210
  3.6 0.8 collective-permute-done.other_ref
  4.4 0.2 fold_queries.1
  4.7 1.2 copy-done
  5.9 13.4 %all-to-all-start = ((bf16[32,224,128]{2,1,0:T(8,128)(2,1)}), bf16[32,224,128]{2,1,0:T(8,128)(2,1)S(1)}, u32[]{:S(2)}, u32[]{:S(2)}) async-start(bf16[32,224,128]{2,1,0:T(8,128)(2,1)} %copy-done), calls=%async_computation | async-start | bytes 3670016 | tf_op jit(solution)/shard_map/all_to_all | solution.py:223
  19.3 1.5 copy.16
  20.8 2.3 %copy.17 = bf16[8,128,448]{2,1,0:T(8,128)(2,1)} copy(bf16[8,128,448]{1,2,0:T(8,128)(2,1)} %param.13) | data formatting | bytes 1835008 | tf_op args[4]
  23.1 1.5 pad_maximum_fusion
  24.7 1.4 broadcast_select_fusion
  26.1 2.4 %copy.18 = bf16[2176,224]{0,1:T(8,128)(2,1)} copy(bf16[2176,224]{1,0:T(8,128)(2,1)} %get-tuple-element.9) | data formatting | bytes 1949696 | tf_op jit(solution)/shard_map/jit(_where)/select_n | solution.py:198
  28.4 2.8 %collective-permute-start.1 = (bf16[2176,224]{0,1:T(8,128)(2,1)}, bf16[2176,224]{0,1:T(8,128)(2,1)}, u32[]{:S(2)}, u32[]{:S(2)}) collective-permute-start(bf16[2176,224]{0,1:T(8,128)(2,1)} %copy.18), channel_id=1, source_target_pairs={{0,8},{8,0},{16,24},{24,16},{32,40},{40,32},{48,56},{56,48},{64,72... | collective-permute-start | bytes 2924552 | tf_op jit(solution)/shard_map/ppermute | solution.py:205
  32.2 1.5 collective-permute-done.1
  33.8 2.3 %copy.19.other_ref = bf16[2176,224]{1,0:T(8,128)(2,1)} copy(bf16[2176,224]{0,1:T(8,128)(2,1)} %collective-permute-done.1) | data formatting | bytes 1949696 | tf_op jit(solution)/shard_map/ppermute | solution.py:205
  36.1 27.8 %all-to-all-done.q_ref = bf16[32,224,128]{2,1,0:T(8,128)(2,1)S(1)} async-done(((bf16[32,224,128]{2,1,0:T(8,128)(2,1)}), bf16[32,224,128]{2,1,0:T(8,128)(2,1)S(1)}, u32[]{:S(2)}, u32[]{:S(2)}) %all-to-all-start) | async-done | bytes 1835040 | tf_op jit(solution)/shard_map/all_to_all | solution.py:223
  63.9 1.2 copy-done.1
  65.1 15.2 %attend.1 = bf16[64,64,256]{2,1,0:T(8,128)(2,1)S(1)} custom-call(s32[18]{0:T(128)S(1)} %pad_add_fusion.2.req, s32[18]{0:T(128)S(1)} %concatenate.17.fill, s32[18]{0:T(128)S(1)} %concatenate.18.off, s32[64]{0:T(128)S(1)} %select_reduce_fusion.inv, bf16[32,224,128]{2,1,0:T(8,128)(2,1)S(1)} %all-to-all-done.q_ref, ...), custom_call_target="tpu_custom_call" | custom-call | tf_op jit(solution)/shard_map/attend/pallas_call | solution.py:244
  80.3 54.5 %all_to_all.15.x_ref = bf16[32,128,256]{2,1,0:T(8,128)(2,1)S(1)} all-to-all(bf16[32,128,256]{2,1,0:T(8,128)(2,1)S(1)} %bitcast.6), channel_id=1, replica_groups={{0,16,32,48,64,80,96,112,128,144,160,176,192,208,224,240,256,272,288,30..., dimensions={0} | all-to-all | bytes 4194304 | tf_op jit(solution)/shard_map/all_to_all | solution.py:263
  134.8 2.8 %merge.1 = (bf16[64,224]{1,0:T(8,128)(2,1)S(1)}, bf16[64,224]{1,0:T(8,128)(2,1)S(1)}) custom-call(s32[1]{0:T(128)} %bitcast.core, bf16[32,128,256]{2,1,0:T(8,128)(2,1)S(1)} %all_to_all.15.x_ref), custom_call_target="tpu_custom_call" | custom-call | tf_op jit(solution)/shard_map/merge/pallas_call | solution.py:272
  137.6 5.0 %collective-permute-start.2 = (bf16[64,224]{1,0:T(8,128)(2,1)S(1)}, bf16[64,224]{1,0:T(8,128)(2,1)S(1)}, u32[]{:S(2)}, u32[]{:S(2)}) collective-permute-start(bf16[64,224]{1,0:T(8,128)(2,1)S(1)} %get-tuple-element.8), channel_id=1, source_target_pairs={{0,8},{8,0},{16,24},{24,16},{32,40},{40,32},{48,56},{56,48},{64,72... | collective-permute-start | bytes 86024 | tf_op jit(solution)/shard_map/ppermute | solution.py:285
  142.6 0.8 collective-permute-done.2.other_ref
  143.5 0.8 project.1
  144.2 26.4 %all_to_all.16 = bf16[8,64,448]{2,1,0:T(8,128)(2,1)S(1)} all-to-all(bf16[8,64,448]{2,1,0:T(8,128)(2,1)S(1)} %project.1), channel_id=1, replica_groups=mesh['blk'=64,'head'=8] {'head'}, dimensions={0} | all-to-all | bytes 917504 | tf_op jit(solution)/shard_map/all_to_all | solution.py:294
  170.7 0.7 reduce_sum.52
  (27 shorter events, 1.0 us)
Async XLA Ops:
  1.0 3.4 %collective-permute-start = (bf16[64,224]{1,0:T(8,128)(2,1)S(1)}, bf16[64,224]{1,0:T(8,128)(2,1)S(1)}, u32[]{:S(2)}, u32[]{:S(2)}) collective-permute-start(bf16[64,224]{1,0:T(8,128)(2,1)S(1)} %get-tuple-element.11), channel_id=1, source_target_pairs={{0,8},{8,0},{16,24},{24,16},{32,40},{40,32},{48,56},{56,48},{64,72... | collective-permute-start | bytes 86024 | tf_op jit(solution)/shard_map/ppermute | solution.py:210
  4.6 1.3 copy-start
  5.9 58.0 %all-to-all-start = ((bf16[32,224,128]{2,1,0:T(8,128)(2,1)}), bf16[32,224,128]{2,1,0:T(8,128)(2,1)S(1)}, u32[]{:S(2)}, u32[]{:S(2)}) async-start(bf16[32,224,128]{2,1,0:T(8,128)(2,1)} %copy-done), calls=%async_computation | async-start | bytes 3670016 | tf_op jit(solution)/shard_map/all_to_all | solution.py:223
  19.3 3.8 %copy-start.3 = (bf16[64,448]{1,0:T(8,128)(2,1)S(1)}, bf16[64,448]{1,0:T(8,128)(2,1)}, u32[]{:S(2)}) copy-start(bf16[64,448]{1,0:T(8,128)(2,1)} %param.11) | copy-start | bytes 172036
  19.3 3.8 %copy-start.4 = (bf16[64,448]{1,0:T(8,128)(2,1)S(1)}, bf16[64,448]{1,0:T(8,128)(2,1)}, u32[]{:S(2)}) copy-start(bf16[64,448]{1,0:T(8,128)(2,1)} %param.10) | copy-start | bytes 172036
  24.6 6.7 %copy-start.5 = (s32[512]{0:T(512)S(1)}, s32[512]{0:T(512)}, u32[]{:S(2)}) copy-start(s32[512]{0:T(512)} %param.16) | copy-start | bytes 6148
  24.6 6.9 %copy-start.6 = (s32[4]{0:T(128)S(1)}, s32[4]{0:T(128)}, u32[]{:S(2)}) copy-start(s32[4]{0:T(128)} %param.15) | copy-start | bytes 52
  24.6 7.1 %copy-start.7 = (s32[64]{0:T(128)S(1)}, s32[64]{0:T(128)}, u32[]{:S(2)}) copy-start(s32[64]{0:T(128)} %param.17) | copy-start | bytes 772
  28.4 5.3 %collective-permute-start.1 = (bf16[2176,224]{0,1:T(8,128)(2,1)}, bf16[2176,224]{0,1:T(8,128)(2,1)}, u32[]{:S(2)}, u32[]{:S(2)}) collective-permute-start(bf16[2176,224]{0,1:T(8,128)(2,1)} %copy.18), channel_id=1, source_target_pairs={{0,8},{8,0},{16,24},{24,16},{32,40},{40,32},{48,56},{56,48},{64,72... | collective-permute-start | bytes 2924552 | tf_op jit(solution)/shard_map/ppermute | solution.py:205
  63.9 1.2 copy-start.1
  80.3 63.2 %copy-start.2 = (bf16[448,3584]{1,0:T(8,128)(2,1)S(1)}, bf16[448,3584]{1,0:T(8,128)(2,1)}, u32[]{:S(2)}) copy-start(bf16[448,3584]{1,0:T(8,128)(2,1)} %w_ref.1) | copy-start | bytes 9633796
  137.6 5.9 %collective-permute-start.2 = (bf16[64,224]{1,0:T(8,128)(2,1)S(1)}, bf16[64,224]{1,0:T(8,128)(2,1)S(1)}, u32[]{:S(2)}, u32[]{:S(2)}) collective-permute-start(bf16[64,224]{1,0:T(8,128)(2,1)S(1)} %get-tuple-element.8), channel_id=1, source_target_pairs={{0,8},{8,0},{16,24},{24,16},{32,40},{40,32},{48,56},{56,48},{64,72... | collective-permute-start | bytes 86024 | tf_op jit(solution)/shard_map/ppermute | solution.py:285
